TPU v7x, 32 devices: a whole 2x2x4 slice. The times are simulated.
32 devices in a mesh: grp: 2 (over x), seq: 8 (over z, y), mdl: 2 (over core).
Axes of the slice: x: 2, y: 2, z: 4, core: 2. Of those that a mesh axis runs over, the one named last changes fastest.
Arguments:
- signal: float32 [8, 128, 8192], P('grp', 'mdl', 'seq'), parts along dimension 0, may hold values from -6 to 6
- lengths: int32 [8], P('grp'), parts along dimension 0, may hold values from 1 to 64, 160 in all
- chan_weight: bfloat16 [128, 128, 16], P('mdl'), may hold values from -0.5 to 0.5
- up_weight: bfloat16 [4, 2048, 4096], P(None, 'seq', 'mdl'), may hold values from -0.125 to 0.125
- down_weight: bfloat16 [4, 2048, 4096], P(None, 'seq', 'mdl'), may hold values from -0.09375 to 0.09375
Outputs:
- features: bfloat16 [8, 64, 2048], P(('grp', 'mdl'), 'seq'), parts along dimension 0
There are 2 independent parts, one for each index of `grp`. A program takes and returns all parts, laid end to end along the dimension named above; an argument that names none is the same for every part. Nothing has to cross between parts.
Inputs may be any that keep to these rules, and one draw needn't show every extreme that they name: `lengths`: live windows of each recording; one recording is live for all 64, and all recordings together have (320) // 2.
All inputs are finite; a program needn't handle non-finite values.
Results may differ from a plain program's by a relative error of at most 0.014.
Values may be sent and summed in bfloat16 or wider, within the bound.
A program may use at most 128 MiB of HBM per device.

v0:
```python
import math
import jax
import jax.numpy as jnp
from jax import lax
from jax.sharding import PartitionSpec as P

HOP = 128
EPSILON = 1e-06


def shifted(x, axis, by):
    size = lax.axis_size(axis)
    pairs = [(i, i + by) for i in range(size) if 0 <= i + by < size]
    return lax.ppermute(x, axis, pairs)


def shifted_2(value, axis, steps):
    count = lax.axis_size(axis)
    pairs = [(source, (source + steps) % count) for source in range(count)]
    return lax.ppermute(value, axis, pairs)


def spectral_table(half_span):
    full_span = 2 * half_span
    row_index = jnp.arange(full_span, dtype=jnp.int32)
    col_index = jnp.arange(half_span, dtype=jnp.int32)
    phases = row_index[:, None] * col_index[None, :] % full_span
    angles = phases.astype(jnp.float32) * (2.0 * math.pi / full_span)
    window_taper = 0.5 - 0.5 * jnp.cos(row_index.astype(jnp.float32) * (2.0 * math.pi / full_span))
    weighting = window_taper * (1.0 / math.sqrt(full_span))
    joined = jnp.concatenate([jnp.cos(angles), -jnp.sin(angles)], axis=1) * weighting[:, None]
    return jnp.concatenate([joined[:half_span], joined[half_span:]], axis=1)


def log_power(spectrum):
    half_span = spectrum.shape[-1] // 2
    real_part = spectrum[..., :half_span]
    imag_part = spectrum[..., half_span:]
    return jnp.log1p(real_part * real_part + imag_part * imag_part).astype(jnp.bfloat16)


def normalize(state_rows):
    values = state_rows.astype(jnp.float32)
    scaled = values * lax.rsqrt(jnp.mean(values * values, axis=1, keepdims=True) + EPSILON)
    return (values, scaled.astype(jnp.bfloat16))


def project_down(hidden, own_down):
    return lax.dot_general(
        hidden, own_down, (((1,), (1,)), ((), ())), preferred_element_type=jnp.float32
    )


def apply_layer(state_rows, own_up, own_down):
    values, normed = normalize(state_rows)
    hidden = jax.nn.gelu(jnp.dot(normed, own_up, preferred_element_type=jnp.float32)).astype(
        jnp.bfloat16
    )
    summed = lax.psum(project_down(hidden, own_down), "mdl")
    return (values + summed).astype(jnp.bfloat16)


def body(signal, lengths, chan_weight, up_weight, down_weight):
    streams, channels, samples = signal.shape
    frames = samples // HOP
    dft_table = spectral_table(HOP)
    boundary = shifted(signal[:, :, :HOP], "seq", -1)
    local_part = jnp.dot(
        signal.reshape(streams, channels, frames, HOP), dft_table, precision=lax.Precision.HIGHEST
    )
    edge_part = jnp.dot(boundary, dft_table[:, 2 * HOP :], precision=lax.Precision.HIGHEST)
    following = jnp.concatenate([local_part[:, :, 1:, 2 * HOP :], edge_part[:, :, None, :]], axis=2)
    spectrum = local_part[..., : 2 * HOP] + following
    logpower = log_power(spectrum)
    embedded = jnp.einsum(
        "scfb,cbe->sfce", logpower, chan_weight, preferred_element_type=jnp.float32
    )
    embedded = embedded.reshape(streams, frames, channels * chan_weight.shape[2])
    frame_index = lax.axis_index("seq") * frames + jnp.arange(frames, dtype=jnp.int32)
    live_mask = frame_index[None, :] < lengths[:, None]
    tokens = jnp.where(live_mask[:, :, None], embedded, 0.0).astype(jnp.bfloat16)
    layer_count = up_weight.shape[0]
    group_size = lax.axis_size("seq") // layer_count
    own_up, own_down = (
        lax.all_to_all(
            jnp.repeat(up_weight, group_size, axis=0),
            "seq",
            split_axis=0,
            concat_axis=1,
            tiled=True,
        ),
        lax.all_to_all(
            jnp.repeat(down_weight, group_size, axis=0),
            "seq",
            split_axis=0,
            concat_axis=1,
            tiled=True,
        ),
    )
    own_up = own_up[0]
    own_down = own_down[0]
    layer_index = lax.axis_index("seq") // group_size
    state_rows = lax.all_gather(tokens, "mdl", axis=2, tiled=True)
    kept_shape = state_rows.shape
    state_rows = state_rows.reshape(kept_shape[0] * kept_shape[1], kept_shape[2])
    for turn_number in range(2 * layer_count):
        if turn_number < 2 * layer_count - 1:
            offset = turn_number - layer_index
            active = (offset >= 0) & (offset < layer_count)
            state_rows = jnp.where(active, apply_layer(state_rows, own_up, own_down), state_rows)
        state_rows = shifted_2(state_rows, "seq", group_size)
    full_rows = state_rows.reshape(kept_shape)
    half_streams = kept_shape[0] // lax.axis_size("mdl")
    return lax.dynamic_slice_in_dim(
        full_rows, lax.axis_index("mdl") * half_streams, half_streams, 0
    )


def solution(mesh):
    return jax.shard_map(
        body,
        mesh=mesh,
        in_specs=(
            P("grp", "mdl", "seq"),
            P("grp"),
            P("mdl", None, None),
            P(None, "seq", "mdl"),
            P(None, "seq", "mdl"),
        ),
        out_specs=P(("grp", "mdl"), "seq", None),
        check_vma=False,
    )
```

profile of v0, /device:TPU:0, one launch (start us, length us, event | category | flops | bytes accessed | tf_op | source)
XLA Modules:
  0.0 677.4 jit_solution(12882907544633261924)
XLA Ops:
  6.5 6.8 %broadcast_in_dim.22 = bf16[4,2,256,2048]{3,2,1,0:T(8,128)(2,1)} broadcast(bf16[4,256,2048]{2,1,0:T(8,128)(2,1)} %param.9), dimensions={0,2,3} | broadcast | bytes 12582912 | tf_op jit(solution)/shard_map/broadcast_in_dim | solution.py:93
  13.3 190.7 %all_to_all.8 = bf16[8,256,2048]{2,1,0:T(8,128)(2,1)} all-to-all(bf16[8,256,2048]{2,1,0:T(8,128)(2,1)} %bitcast.67), channel_id=1, replica_groups=mesh['grp'=2,'seq'=8,'mdl'=2] {'seq'}, dimensions={0} | all-to-all | bytes 16777216 | tf_op jit(solution)/shard_map/all_to_all | solution.py:92
  204.0 4.3 broadcast_in_dim.21
  208.3 5.2 all-to-all-start
  213.6 1.3 collective-permute-start
  214.9 0.5 sine_negate_fusion
  215.5 0.1 maximum_multiply_fusion
  215.6 3.5 convolution_bitcast_fusion
  219.2 2.0 copy-done.1
  221.1 0.2 slice.31
  221.4 42.6 %collective-permute-done = f32[4,64,128]{2,1,0:T(8,128)S(1)} collective-permute-done((f32[4,64,128]{2,1,0:T(8,128)S(1)}, f32[4,64,128]{2,1,0:T(8,128)S(1)}, u32[]{:S(2)}, u32[]{:S(2)}) %collective-permute-start) | collective-permute-done | bytes 131104 | tf_op jit(solution)/shard_map/ppermute | solution.py:14
  264.0 0.4 convolution_bitcast_fusion.2
  264.4 1.9 slice_add_fusion
  266.3 0.4 fusion.4
  266.8 0.4 convolution_bitcast_fusion.1
  267.2 0.2 copy.10
  267.4 0.8 reshape.133
  268.2 1.9 all_gather.3
  270.1 0.1 fusion.6
  270.3 126.8 %all-to-all-done = bf16[8,256,2048]{2,1,0:T(8,128)(2,1)} async-done(((bf16[8,256,2048]{2,1,0:T(8,128)(2,1)}), bf16[8,256,2048]{2,1,0:T(8,128)(2,1)}, u32[]{:S(2)}, u32[]{:S(2)}) %all-to-all-start) | async-done | bytes 8388640 | tf_op jit(solution)/shard_map/all_to_all | solution.py:85
  397.1 10.6 %fusion.143 = f32[32,2048]{1,0:T(8,128)} fusion(bf16[2048,2048]{1,0:T(8,128)(2,1)} %bitcast.59, bf16[2048,2048]{1,0:T(8,128)(2,1)} %bitcast.12, bf16[4,8,2048]{2,1,0:T(8,128)(2,1)S(1)} %all_gather.3, f32[4,8]{1,0:T(4,128)S(1)} %add_rsqrt_fusion), kind=kOutput, calls=%fused_computation.146 | convolution fusion | flops 537657344 | bytes 17170560 | tf_op jit(solution)/shard_map/dot_general | solution.py:49
  407.7 0.2 all-reduce.10.cloned.1.call-start
  407.9 23.9 %all-reduce.8.cloned.1.call-done = f32[32,2048]{1,0:T(8,128)} async-done(((f32[32,2048]{1,0:T(8,128)}), f32[32,2048]{1,0:T(8,128)}) %all-reduce.8.cloned.1.call-update) | async-done | bytes 262160 | tf_op jit(solution)/shard_map/psum | solution.py:59
  431.8 1.0 fusion.85
  432.8 1.8 collective-permute-start.1
  434.6 5.8 collective-permute-done.1
  440.4 0.1 fusion.16
  440.6 10.6 %fusion.135 = f32[32,2048]{1,0:T(8,128)} fusion(bf16[2048,2048]{1,0:T(8,128)(2,1)} %bitcast.60, bf16[2048,2048]{1,0:T(8,128)(2,1)} %bitcast.12, bf16[32,2048]{1,0:T(8,128)(2,1)S(1)} %collective-permute-done.1, f32[32]{0:T(128)S(1)} %add_rsqrt_fusion.6), kind=kOutput, calls=%fused_computation.144 | convolution fusion | flops 537657344 | bytes 17170560 | tf_op jit(solution)/shard_map/dot_general | solution.py:49
  451.2 17.7 %all-reduce.10.cloned.1.call-done = f32[32,2048]{1,0:T(8,128)} async-done(((f32[32,2048]{1,0:T(8,128)}), f32[32,2048]{1,0:T(8,128)}) %all-reduce.10.cloned.1.call-update) | async-done | bytes 262160 | tf_op jit(solution)/shard_map/psum | solution.py:59
  468.9 1.0 fusion.91
  469.9 1.8 collective-permute-start.2
  471.7 5.8 collective-permute-done.2
  477.5 0.1 fusion.27
  477.7 10.6 %fusion.127 = f32[32,2048]{1,0:T(8,128)} fusion(bf16[2048,2048]{1,0:T(8,128)(2,1)} %bitcast.61, bf16[2048,2048]{1,0:T(8,128)(2,1)} %bitcast.12, bf16[32,2048]{1,0:T(8,128)(2,1)S(1)} %collective-permute-done.2, f32[32]{0:T(128)S(1)} %add_rsqrt_fusion.5), kind=kOutput, calls=%fused_computation.142 | convolution fusion | flops 537657344 | bytes 17170560 | tf_op jit(solution)/shard_map/dot_general | solution.py:49
  488.3 17.7 %all-reduce.12.cloned.1.call-done = f32[32,2048]{1,0:T(8,128)} async-done(((f32[32,2048]{1,0:T(8,128)}), f32[32,2048]{1,0:T(8,128)}) %all-reduce.12.cloned.1.call-update) | async-done | bytes 262160 | tf_op jit(solution)/shard_map/psum | solution.py:59
  506.0 1.0 fusion.90
  507.0 1.8 collective-permute-start.3
  508.8 5.8 collective-permute-done.3
  514.6 0.1 fusion.38
  514.7 10.6 %fusion.119 = f32[32,2048]{1,0:T(8,128)} fusion(bf16[2048,2048]{1,0:T(8,128)(2,1)} %bitcast.62, bf16[2048,2048]{1,0:T(8,128)(2,1)} %bitcast.12, bf16[32,2048]{1,0:T(8,128)(2,1)S(1)} %collective-permute-done.3, f32[32]{0:T(128)S(1)} %add_rsqrt_fusion.4), kind=kOutput, calls=%fused_computation.140 | convolution fusion | flops 537657344 | bytes 17170560 | tf_op jit(solution)/shard_map/dot_general | solution.py:49
  525.4 17.7 %all-reduce.14.cloned.1.call-done = f32[32,2048]{1,0:T(8,128)} async-done(((f32[32,2048]{1,0:T(8,128)}), f32[32,2048]{1,0:T(8,128)}) %all-reduce.14.cloned.1.call-update) | async-done | bytes 262160 | tf_op jit(solution)/shard_map/psum | solution.py:59
  543.1 1.0 fusion.89
  544.1 2.0 collective-permute-start.4
  546.1 5.8 collective-permute-done.4
  551.9 0.1 fusion.49
  552.0 10.6 %fusion.111 = f32[32,2048]{1,0:T(8,128)} fusion(bf16[2048,2048]{1,0:T(8,128)(2,1)} %bitcast.63, bf16[2048,2048]{1,0:T(8,128)(2,1)} %bitcast.12, bf16[32,2048]{1,0:T(8,128)(2,1)S(1)} %collective-permute-done.4, f32[32]{0:T(128)S(1)} %add_rsqrt_fusion.3), kind=kOutput, calls=%fused_computation.138 | convolution fusion | flops 537657344 | bytes 17170560 | tf_op jit(solution)/shard_map/dot_general | solution.py:49
  562.7 17.7 %all-reduce.16.cloned.1.call-done = f32[32,2048]{1,0:T(8,128)} async-done(((f32[32,2048]{1,0:T(8,128)}), f32[32,2048]{1,0:T(8,128)}) %all-reduce.16.cloned.1.call-update) | async-done | bytes 262160 | tf_op jit(solution)/shard_map/psum | solution.py:59
  580.4 1.0 fusion.88
  581.4 1.8 collective-permute-start.5
  583.2 5.8 collective-permute-done.5
  589.0 0.1 fusion.60
  589.1 10.6 %fusion.103 = f32[32,2048]{1,0:T(8,128)} fusion(bf16[2048,2048]{1,0:T(8,128)(2,1)} %bitcast.64, bf16[2048,2048]{1,0:T(8,128)(2,1)} %bitcast.12, bf16[32,2048]{1,0:T(8,128)(2,1)S(1)} %collective-permute-done.5, f32[32]{0:T(128)S(1)} %add_rsqrt_fusion.2), kind=kOutput, calls=%fused_computation.136 | convolution fusion | flops 537657344 | bytes 17170560 | tf_op jit(solution)/shard_map/dot_general | solution.py:49
  599.8 17.7 %all-reduce.18.cloned.1.call-done = f32[32,2048]{1,0:T(8,128)} async-done(((f32[32,2048]{1,0:T(8,128)}), f32[32,2048]{1,0:T(8,128)}) %all-reduce.18.cloned.1.call-update) | async-done | bytes 262160 | tf_op jit(solution)/shard_map/psum | solution.py:59
  617.5 1.0 fusion.87
  618.5 1.8 collective-permute-start.6
  620.3 5.8 collective-permute-done.6
  626.1 0.1 fusion.71
  626.2 10.6 %fusion.95 = f32[32,2048]{1,0:T(8,128)} fusion(bf16[2048,2048]{1,0:T(8,128)(2,1)} %bitcast.65, bf16[2048,2048]{1,0:T(8,128)(2,1)} %bitcast.12, bf16[32,2048]{1,0:T(8,128)(2,1)S(1)} %collective-permute-done.6, f32[32]{0:T(128)S(1)} %add_rsqrt_fusion.1), kind=kOutput, calls=%fused_computation.134 | convolution fusion | flops 537657344 | bytes 17170560 | tf_op jit(solution)/shard_map/dot_general | solution.py:49
  636.8 17.7 %all-reduce.20.cloned.1.call-done = f32[32,2048]{1,0:T(8,128)} async-done(((f32[32,2048]{1,0:T(8,128)}), f32[32,2048]{1,0:T(8,128)}) %all-reduce.20.cloned.1.call-update) | async-done | bytes 262160 | tf_op jit(solution)/shard_map/psum | solution.py:59
  654.6 1.0 fusion.86
  655.5 1.8 collective-permute-start.7
  657.3 5.8 collective-permute-done.7
  663.1 6.8 collective-permute-done.8
  669.9 0.6 constant_dynamic-slice_fusion
  (36 shorter events, 0.7 us)
Async XLA Ops:
  6.5 260.2 %copy-start = (bf16[64,128,16]{1,2,0:T(8,128)(2,1)S(1)}, bf16[64,128,16]{1,2,0:T(8,128)(2,1)}, u32[]{:S(2)}) copy-start(bf16[64,128,16]{1,2,0:T(8,128)(2,1)} %param.7) | copy-start | bytes 786436
  13.3 190.7 %copy-start.2 = (bf16[4,256,2048]{2,1,0:T(8,128)(2,1)S(1)}, bf16[4,256,2048]{2,1,0:T(8,128)(2,1)}, u32[]{:S(2)}) copy-start(bf16[4,256,2048]{2,1,0:T(8,128)(2,1)} %param.8) | copy-start | bytes 12582916
  208.3 5.2 copy-start.3
  208.3 188.8 %all-to-all-start = ((bf16[8,256,2048]{2,1,0:T(8,128)(2,1)}), bf16[8,256,2048]{2,1,0:T(8,128)(2,1)}, u32[]{:S(2)}, u32[]{:S(2)}) async-start(bf16[8,256,2048]{2,1,0:T(8,128)(2,1)} %bitcast.66), calls=%async_computation | async-start | bytes 16777216 | tf_op jit(solution)/shard_map/all_to_all | solution.py:85
  213.5 7.9 %copy-start.4 = (s32[4]{0:T(128)S(1)}, s32[4]{0:T(128)}, u32[]{:S(2)}) copy-start(s32[4]{0:T(128)} %param.6) | copy-start | bytes 52
  213.5 218.4 %all-reduce.8.cloned.1.call-start = ((), (), s32[]{:S(2)}) async-start(), calls=%async_computation.2 | async-start | bytes 524288 | tf_op jit(solution)/shard_map/psum | solution.py:59
  213.6 50.4 %collective-permute-start = (f32[4,64,128]{2,1,0:T(8,128)S(1)}, f32[4,64,128]{2,1,0:T(8,128)S(1)}, u32[]{:S(2)}, u32[]{:S(2)}) collective-permute-start(f32[4,64,128]{2,1,0:T(8,128)S(1)} %slice.25), channel_id=1, source_target_pairs={{2,0},{4,2},{6,4},{8,6},{10,8},{12,10},{14,12},{3,1},{5,3},{7,5},{... | collective-permute-start | bytes 393224 | tf_op jit(solution)/shard_map/ppermute | solution.py:14
  219.2 2.0 copy-start.1
  407.7 61.3 %all-reduce.10.cloned.1.call-start = ((), (), s32[]{:S(2)}) async-start(), calls=%async_computation.3 | async-start | bytes 524288 | tf_op jit(solution)/shard_map/psum | solution.py:59
  432.8 7.6 %collective-permute-start.1 = (bf16[32,2048]{1,0:T(8,128)(2,1)S(1)}, bf16[32,2048]{1,0:T(8,128)(2,1)S(1)}, u32[]{:S(2)}, u32[]{:S(2)}) collective-permute-start(bf16[32,2048]{1,0:T(8,128)(2,1)S(1)} %fusion.85), channel_id=1, source_target_pairs={{0,4},{2,6},{4,8},{6,10},{8,12},{10,14},{12,0},{14,2},{1,5},{3,7},... | collective-permute-start | bytes 393224 | tf_op jit(solution)/shard_map/ppermute | solution.py:20
  451.2 54.8 %all-reduce.12.cloned.1.call-start = ((), (), s32[]{:S(2)}) async-start(), calls=%async_computation.4 | async-start | bytes 524288 | tf_op jit(solution)/shard_map/psum | solution.py:59
  469.9 7.6 %collective-permute-start.2 = (bf16[32,2048]{1,0:T(8,128)(2,1)S(1)}, bf16[32,2048]{1,0:T(8,128)(2,1)S(1)}, u32[]{:S(2)}, u32[]{:S(2)}) collective-permute-start(bf16[32,2048]{1,0:T(8,128)(2,1)S(1)} %fusion.91), channel_id=1, source_target_pairs={{0,4},{2,6},{4,8},{6,10},{8,12},{10,14},{12,0},{14,2},{1,5},{3,7},... | collective-permute-start | bytes 393224 | tf_op jit(solution)/shard_map/ppermute | solution.py:20
  488.3 54.8 %all-reduce.14.cloned.1.call-start = ((), (), s32[]{:S(2)}) async-start(), calls=%async_computation.5 | async-start | bytes 524288 | tf_op jit(solution)/shard_map/psum | solution.py:59
  507.0 7.6 %collective-permute-start.3 = (bf16[32,2048]{1,0:T(8,128)(2,1)S(1)}, bf16[32,2048]{1,0:T(8,128)(2,1)S(1)}, u32[]{:S(2)}, u32[]{:S(2)}) collective-permute-start(bf16[32,2048]{1,0:T(8,128)(2,1)S(1)} %fusion.90), channel_id=1, source_target_pairs={{0,4},{2,6},{4,8},{6,10},{8,12},{10,14},{12,0},{14,2},{1,5},{3,7},... | collective-permute-start | bytes 393224 | tf_op jit(solution)/shard_map/ppermute | solution.py:20
  525.4 55.0 %all-reduce.16.cloned.1.call-start = ((), (), s32[]{:S(2)}) async-start(), calls=%async_computation.6 | async-start | bytes 524288 | tf_op jit(solution)/shard_map/psum | solution.py:59
  544.1 7.8 %collective-permute-start.4 = (bf16[32,2048]{1,0:T(8,128)(2,1)S(1)}, bf16[32,2048]{1,0:T(8,128)(2,1)S(1)}, u32[]{:S(2)}, u32[]{:S(2)}) collective-permute-start(bf16[32,2048]{1,0:T(8,128)(2,1)S(1)} %fusion.89), channel_id=1, source_target_pairs={{0,4},{2,6},{4,8},{6,10},{8,12},{10,14},{12,0},{14,2},{1,5},{3,7},... | collective-permute-start | bytes 393224 | tf_op jit(solution)/shard_map/ppermute | solution.py:20
  562.7 54.8 %all-reduce.18.cloned.1.call-start = ((), (), s32[]{:S(2)}) async-start(), calls=%async_computation.7 | async-start | bytes 524288 | tf_op jit(solution)/shard_map/psum | solution.py:59
  581.4 7.6 %collective-permute-start.5 = (bf16[32,2048]{1,0:T(8,128)(2,1)S(1)}, bf16[32,2048]{1,0:T(8,128)(2,1)S(1)}, u32[]{:S(2)}, u32[]{:S(2)}) collective-permute-start(bf16[32,2048]{1,0:T(8,128)(2,1)S(1)} %fusion.88), channel_id=1, source_target_pairs={{0,4},{2,6},{4,8},{6,10},{8,12},{10,14},{12,0},{14,2},{1,5},{3,7},... | collective-permute-start | bytes 393224 | tf_op jit(solution)/shard_map/ppermute | solution.py:20
  599.7 54.8 %all-reduce.20.cloned.1.call-start = ((), (), s32[]{:S(2)}) async-start(), calls=%async_computation.8 | async-start | bytes 524288 | tf_op jit(solution)/shard_map/psum | solution.py:59
  618.5 7.6 %collective-permute-start.6 = (bf16[32,2048]{1,0:T(8,128)(2,1)S(1)}, bf16[32,2048]{1,0:T(8,128)(2,1)S(1)}, u32[]{:S(2)}, u32[]{:S(2)}) collective-permute-start(bf16[32,2048]{1,0:T(8,128)(2,1)S(1)} %fusion.87), channel_id=1, source_target_pairs={{0,4},{2,6},{4,8},{6,10},{8,12},{10,14},{12,0},{14,2},{1,5},{3,7},... | collective-permute-start | bytes 393224 | tf_op jit(solution)/shard_map/ppermute | solution.py:20
  655.5 7.6 %collective-permute-start.7 = (bf16[32,2048]{1,0:T(8,128)(2,1)S(1)}, bf16[32,2048]{1,0:T(8,128)(2,1)S(1)}, u32[]{:S(2)}, u32[]{:S(2)}) collective-permute-start(bf16[32,2048]{1,0:T(8,128)(2,1)S(1)} %fusion.86), channel_id=1, source_target_pairs={{0,4},{2,6},{4,8},{6,10},{8,12},{10,14},{12,0},{14,2},{1,5},{3,7},... | collective-permute-start | bytes 393224 | tf_op jit(solution)/shard_map/ppermute | solution.py:20
  663.1 6.8 collective-permute-start.8
Sparse Core Ops, SparseCore 0:
  407.8 24.0 all-reduce.7
  451.3 17.5 all-reduce.9
  488.4 17.5 all-reduce.11
  525.5 17.5 all-reduce.13
  562.8 17.5 all-reduce.15
  599.9 17.5 all-reduce.17
  636.9 17.5 all-reduce.19
where the time goes:
time: 678 us; the launch traced here: 677 us
  waiting for transfers between devices  347 us (51%)
  blocking collectives  193 us (28%)
  matrix products  78.4 us (12%)
  starting transfers between devices  19.7 us (3%)
  local copies, waits for them, and re-layouts  14.9 us (2%)
  between operations  13.8 us (2%)
  other arithmetic  11.1 us (2%)
    all_to_all x1, blocking collectives, body(): lax.all_to_all(jnp.repeat(down_weight, group_size, axis=0), 'seq', split_...  191 us
    psum x7, waiting for transfers between devices, apply_layer(): summed = lax.psum(project_down(hidden, own_down), 'mdl')  130 us
    all_to_all x1, waiting for transfers between devices, body(): lax.all_to_all(jnp.repeat(up_weight, group_size, axis=0), 'seq', split_ax...  127 us
    dot_general x7, matrix products, project_down(): lax.dot_general(hidden, own_down, (((1,), (1,)), ((), ())), preferred_ele...  74.1 us
    ppermute x8, waiting for transfers between devices, shifted_2(): return lax.ppermute(value, axis, pairs)  47.4 us
    ppermute x1, waiting for transfers between devices, shifted(): return lax.ppermute(x, axis, pairs)  42.6 us
  transfers between devices with their start and end apart: 17, of which 17 were waited for; matrix products, arithmetic and copies ran while one was open for 1% of the time, Pallas kernels for 0%

commit v1 on v0

--- a/solution.py
+++ b/solution.py
@@ -3,6 +3,7 @@
 import jax.numpy as jnp
 from jax import lax
 from jax.sharding import PartitionSpec as P
+from jax.lax import all_gather
 
 HOP = 128
 EPSILON = 1e-06
@@ -56,7 +57,7 @@
     hidden = jax.nn.gelu(jnp.dot(normed, own_up, preferred_element_type=jnp.float32)).astype(
         jnp.bfloat16
     )
-    summed = lax.psum(project_down(hidden, own_down), "mdl")
+    summed = all_gather(project_down(hidden, own_down), "mdl").sum(axis=0)
     return (values + summed).astype(jnp.bfloat16)
 
 

time: 678 us -> 539 us (0.79)
  waiting for transfers between devices: 347 us -> 225 us
  blocking collectives: 193 us -> 208 us
  between operations: 13.8 us -> 0.35 us
  starting transfers between devices: 19.7 us -> 10.6 us
    psum x7 -> x0, waiting for transfers between devices: 130 us -> none  [apply_layer(): summed = lax.psum(project_down(hidden, own_down), 'mdl')]
    all_gather x0 -> x7, blocking collectives: none -> 15.5 us  [apply_layer(): summed = all_gather(project_down(hidden, own_down), 'mdl').sum(axis=0)]
    ppermute x8, starting transfers between devices: 12.8 us -> 4.12 us  [shifted_2(): return lax.ppermute(value, axis, pairs)]
    ppermute x8, waiting for transfers between devices: 47.4 us -> 56 us  [shifted_2(): return lax.ppermute(value, axis, pairs)]
  transfers between devices with their start and end apart: 17 -> 10, of which waited for: 17 -> 10; matrix products, arithmetic and copies ran while one was open for 1% -> 2% of each run, Pallas kernels for 0% -> 0%
where the time goes in v1:
time: 539 us; the launch traced here: 537 us
  waiting for transfers between devices  225 us (42%)
  blocking collectives  208 us (39%)
  matrix products  73.4 us (14%)
  local copies, waits for them, and re-layouts  14.9 us (3%)
  starting transfers between devices  10.6 us (2%)
    all_to_all x1, blocking collectives, body(): lax.all_to_all(jnp.repeat(down_weight, group_size, axis=0), 'seq', split_...  191 us
    all_to_all x1, waiting for transfers between devices, body(): lax.all_to_all(jnp.repeat(up_weight, group_size, axis=0), 'seq', split_ax...  127 us
    dot_general x7, matrix products, project_down(): lax.dot_general(hidden, own_down, (((1,), (1,)), ((), ())), preferred_ele...  69.1 us
    ppermute x8, waiting for transfers between devices, shifted_2(): return lax.ppermute(value, axis, pairs)  56 us
    ppermute x1, waiting for transfers between devices, shifted(): return lax.ppermute(x, axis, pairs)  42.6 us
    all_gather x7, blocking collectives, apply_layer(): summed = all_gather(project_down(hidden, own_down), 'mdl').sum(axis=0)  15.5 us
  transfers between devices with their start and end apart: 10, of which 10 were waited for; matrix products, arithmetic and copies ran while one was open for 2% of the time, Pallas kernels for 0%

profile of v1, /device:TPU:0, one launch (start us, length us, event | category | flops | bytes accessed | tf_op | source)
XLA Modules:
  0.0 537.4 jit_solution(3900778185091365195)
XLA Ops:
  0.0 0.0 copy-start
  0.0 6.8 %broadcast_in_dim.22 = bf16[4,2,256,2048]{3,2,1,0:T(8,128)(2,1)} broadcast(bf16[4,256,2048]{2,1,0:T(8,128)(2,1)} %param.9), dimensions={0,2,3} | broadcast | bytes 12582912 | tf_op jit(solution)/shard_map/broadcast_in_dim | solution.py:94
  6.8 190.7 %all_to_all.8 = bf16[8,256,2048]{2,1,0:T(8,128)(2,1)} all-to-all(bf16[8,256,2048]{2,1,0:T(8,128)(2,1)} %bitcast.74), channel_id=1, replica_groups=mesh['grp'=2,'seq'=8,'mdl'=2] {'seq'}, dimensions={0} | all-to-all | bytes 16777216 | tf_op jit(solution)/shard_map/all_to_all | solution.py:93
  197.5 0.0 copy-done.2
  197.5 4.3 broadcast_in_dim.21
  201.8 5.2 all-to-all-start
  206.9 0.0 copy-done.3
  207.0 0.0 copy-start.4
  207.0 1.3 collective-permute-start
  208.3 0.5 sine_negate_fusion
  208.9 0.1 maximum_multiply_fusion
  209.0 3.5 convolution_bitcast_fusion
  212.6 2.0 copy-done.1
  214.5 0.2 slice.31
  214.8 0.0 copy-done.4
  214.8 0.1 broadcast_compare_fusion
  214.9 42.6 %collective-permute-done = f32[4,64,128]{2,1,0:T(8,128)S(1)} collective-permute-done((f32[4,64,128]{2,1,0:T(8,128)S(1)}, f32[4,64,128]{2,1,0:T(8,128)S(1)}, u32[]{:S(2)}, u32[]{:S(2)}) %collective-permute-start) | collective-permute-done | bytes 131104 | tf_op jit(solution)/shard_map/ppermute | solution.py:15
  257.5 0.4 convolution_bitcast_fusion.2
  257.9 1.9 slice_add_fusion
  259.8 0.4 fusion.4
  260.2 0.4 convolution_bitcast_fusion.1
  260.6 0.2 copy.10
  260.9 0.8 reshape.133
  261.6 0.1 select_convert_fusion
  261.7 1.9 all_gather.45
  263.6 0.1 fusion.6
  263.7 126.8 %all-to-all-done = bf16[8,256,2048]{2,1,0:T(8,128)(2,1)} async-done(((bf16[8,256,2048]{2,1,0:T(8,128)(2,1)}), bf16[8,256,2048]{2,1,0:T(8,128)(2,1)}, u32[]{:S(2)}, u32[]{:S(2)}) %all-to-all-start) | async-done | bytes 8388640 | tf_op jit(solution)/shard_map/all_to_all | solution.py:86
  390.5 9.9 %fusion.143 = f32[32,2048]{1,0:T(8,128)S(1)} fusion(bf16[2048,2048]{1,0:T(8,128)(2,1)} %bitcast.66, bf16[2048,2048]{1,0:T(8,128)(2,1)} %bitcast.12, bf16[4,8,2048]{2,1,0:T(8,128)(2,1)S(1)} %all_gather.45, f32[4,8]{1,0:T(4,128)S(1)} %add_rsqrt_fusion), kind=kOutput, calls=%fused_computation.146 | convolution fusion | flops 537657344 | bytes 17170560 | tf_op jit(solution)/shard_map/dot_general | solution.py:50
  400.4 2.4 all-gather
  402.8 0.1 collective-permute-start.1
  402.9 7.3 %collective-permute-done.1 = bf16[32,2048]{1,0:T(8,128)(2,1)S(1)} collective-permute-done((bf16[32,2048]{1,0:T(8,128)(2,1)S(1)}, bf16[32,2048]{1,0:T(8,128)(2,1)S(1)}, u32[]{:S(2)}, u32[]{:S(2)}) %collective-permute-start.1) | collective-permute-done | bytes 131104 | tf_op jit(solution)/shard_map/ppermute | solution.py:21
  410.2 0.1 fusion.16
  410.4 9.9 %fusion.135 = f32[32,2048]{1,0:T(8,128)S(1)} fusion(bf16[2048,2048]{1,0:T(8,128)(2,1)} %bitcast.67, bf16[2048,2048]{1,0:T(8,128)(2,1)} %bitcast.12, bf16[32,2048]{1,0:T(8,128)(2,1)S(1)} %collective-permute-done.1, f32[32]{0:T(128)S(1)} %add_rsqrt_fusion.6), kind=kOutput, calls=%fused_computation.144 | convolution fusion | flops 537657344 | bytes 17170560 | tf_op jit(solution)/shard_map/dot_general | solution.py:50
  420.2 2.2 all-gather.1
  422.5 3.4 collective-permute-start.2
  425.9 5.4 %collective-permute-done.2 = bf16[32,2048]{1,0:T(8,128)(2,1)S(1)} collective-permute-done((bf16[32,2048]{1,0:T(8,128)(2,1)S(1)}, bf16[32,2048]{1,0:T(8,128)(2,1)S(1)}, u32[]{:S(2)}, u32[]{:S(2)}) %collective-permute-start.2) | collective-permute-done | bytes 131104 | tf_op jit(solution)/shard_map/ppermute | solution.py:21
  431.4 0.1 fusion.27
  431.5 9.9 %fusion.127 = f32[32,2048]{1,0:T(8,128)S(1)} fusion(bf16[2048,2048]{1,0:T(8,128)(2,1)} %bitcast.68, bf16[2048,2048]{1,0:T(8,128)(2,1)} %bitcast.12, bf16[32,2048]{1,0:T(8,128)(2,1)S(1)} %collective-permute-done.2, f32[32]{0:T(128)S(1)} %add_rsqrt_fusion.5), kind=kOutput, calls=%fused_computation.142 | convolution fusion | flops 537657344 | bytes 17170560 | tf_op jit(solution)/shard_map/dot_general | solution.py:50
  441.4 2.2 all-gather.2
  443.7 0.2 collective-permute-start.3
  443.8 7.2 %collective-permute-done.3 = bf16[32,2048]{1,0:T(8,128)(2,1)S(1)} collective-permute-done((bf16[32,2048]{1,0:T(8,128)(2,1)S(1)}, bf16[32,2048]{1,0:T(8,128)(2,1)S(1)}, u32[]{:S(2)}, u32[]{:S(2)}) %collective-permute-start.3) | collective-permute-done | bytes 131104 | tf_op jit(solution)/shard_map/ppermute | solution.py:21
  451.0 0.1 fusion.38
  451.2 9.9 %fusion.119 = f32[32,2048]{1,0:T(8,128)S(1)} fusion(bf16[2048,2048]{1,0:T(8,128)(2,1)} %bitcast.69, bf16[2048,2048]{1,0:T(8,128)(2,1)} %bitcast.12, bf16[32,2048]{1,0:T(8,128)(2,1)S(1)} %collective-permute-done.3, f32[32]{0:T(128)S(1)} %add_rsqrt_fusion.4), kind=kOutput, calls=%fused_computation.140 | convolution fusion | flops 537657344 | bytes 17170560 | tf_op jit(solution)/shard_map/dot_general | solution.py:50
  461.1 2.2 all-gather.3
  463.3 0.3 collective-permute-start.4
  463.6 7.3 %collective-permute-done.4 = bf16[32,2048]{1,0:T(8,128)(2,1)S(1)} collective-permute-done((bf16[32,2048]{1,0:T(8,128)(2,1)S(1)}, bf16[32,2048]{1,0:T(8,128)(2,1)S(1)}, u32[]{:S(2)}, u32[]{:S(2)}) %collective-permute-start.4) | collective-permute-done | bytes 131104 | tf_op jit(solution)/shard_map/ppermute | solution.py:21
  470.9 0.1 fusion.49
  471.1 9.9 %fusion.111 = f32[32,2048]{1,0:T(8,128)S(1)} fusion(bf16[2048,2048]{1,0:T(8,128)(2,1)} %bitcast.70, bf16[2048,2048]{1,0:T(8,128)(2,1)} %bitcast.12, bf16[32,2048]{1,0:T(8,128)(2,1)S(1)} %collective-permute-done.4, f32[32]{0:T(128)S(1)} %add_rsqrt_fusion.3), kind=kOutput, calls=%fused_computation.138 | convolution fusion | flops 537657344 | bytes 17170560 | tf_op jit(solution)/shard_map/dot_general | solution.py:50
  481.0 2.2 all-gather.4
  483.2 0.1 collective-permute-start.5
  483.3 7.3 %collective-permute-done.5 = bf16[32,2048]{1,0:T(8,128)(2,1)S(1)} collective-permute-done((bf16[32,2048]{1,0:T(8,128)(2,1)S(1)}, bf16[32,2048]{1,0:T(8,128)(2,1)S(1)}, u32[]{:S(2)}, u32[]{:S(2)}) %collective-permute-start.5) | collective-permute-done | bytes 131104 | tf_op jit(solution)/shard_map/ppermute | solution.py:21
  490.6 0.1 fusion.60
  490.8 9.9 %fusion.103 = f32[32,2048]{1,0:T(8,128)S(1)} fusion(bf16[2048,2048]{1,0:T(8,128)(2,1)} %bitcast.71, bf16[2048,2048]{1,0:T(8,128)(2,1)} %bitcast.12, bf16[32,2048]{1,0:T(8,128)(2,1)S(1)} %collective-permute-done.5, f32[32]{0:T(128)S(1)} %add_rsqrt_fusion.2), kind=kOutput, calls=%fused_computation.136 | convolution fusion | flops 537657344 | bytes 17170560 | tf_op jit(solution)/shard_map/dot_general | solution.py:50
  500.6 2.2 all-gather.5
  502.9 0.1 collective-permute-start.6
  503.0 7.3 %collective-permute-done.6 = bf16[32,2048]{1,0:T(8,128)(2,1)S(1)} collective-permute-done((bf16[32,2048]{1,0:T(8,128)(2,1)S(1)}, bf16[32,2048]{1,0:T(8,128)(2,1)S(1)}, u32[]{:S(2)}, u32[]{:S(2)}) %collective-permute-start.6) | collective-permute-done | bytes 131104 | tf_op jit(solution)/shard_map/ppermute | solution.py:21
  510.3 0.1 fusion.71
  510.4 9.9 %fusion.95 = f32[32,2048]{1,0:T(8,128)S(1)} fusion(bf16[2048,2048]{1,0:T(8,128)(2,1)} %bitcast.72, bf16[2048,2048]{1,0:T(8,128)(2,1)} %bitcast.12, bf16[32,2048]{1,0:T(8,128)(2,1)S(1)} %collective-permute-done.6, f32[32]{0:T(128)S(1)} %add_rsqrt_fusion.1), kind=kOutput, calls=%fused_computation.134 | convolution fusion | flops 537657344 | bytes 17170560 | tf_op jit(solution)/shard_map/dot_general | solution.py:50
  520.3 2.2 all-gather.6
  522.6 0.1 collective-permute-start.7
  522.6 7.3 %collective-permute-done.7 = bf16[32,2048]{1,0:T(8,128)(2,1)S(1)} collective-permute-done((bf16[32,2048]{1,0:T(8,128)(2,1)S(1)}, bf16[32,2048]{1,0:T(8,128)(2,1)S(1)}, u32[]{:S(2)}, u32[]{:S(2)}) %collective-permute-start.7) | collective-permute-done | bytes 131104 | tf_op jit(solution)/shard_map/ppermute | solution.py:21
  530.0 0.0 collective-permute-start.8
  530.0 6.8 %collective-permute-done.8 = bf16[32,2048]{1,0:T(8,128)(2,1)S(1)} collective-permute-done((bf16[32,2048]{1,0:T(8,128)(2,1)S(1)}, bf16[32,2048]{1,0:T(8,128)(2,1)S(1)}, u32[]{:S(2)}, u32[]{:S(2)}) %collective-permute-start.8) | collective-permute-done | bytes 131104 | tf_op jit(solution)/shard_map/ppermute | solution.py:21
  536.7 0.6 constant_dynamic-slice_fusion
  (29 shorter events, 0.6 us)
Async XLA Ops:
  0.0 260.2 %copy-start = (bf16[64,128,16]{1,2,0:T(8,128)(2,1)S(1)}, bf16[64,128,16]{1,2,0:T(8,128)(2,1)}, u32[]{:S(2)}) copy-start(bf16[64,128,16]{1,2,0:T(8,128)(2,1)} %param.7) | copy-start | bytes 786436
  6.8 190.7 %copy-start.2 = (bf16[4,256,2048]{2,1,0:T(8,128)(2,1)S(1)}, bf16[4,256,2048]{2,1,0:T(8,128)(2,1)}, u32[]{:S(2)}) copy-start(bf16[4,256,2048]{2,1,0:T(8,128)(2,1)} %param.8) | copy-start | bytes 12582916
  201.8 5.2 copy-start.3
  201.8 188.8 %all-to-all-start = ((bf16[8,256,2048]{2,1,0:T(8,128)(2,1)}), bf16[8,256,2048]{2,1,0:T(8,128)(2,1)}, u32[]{:S(2)}, u32[]{:S(2)}) async-start(bf16[8,256,2048]{2,1,0:T(8,128)(2,1)} %bitcast.73), calls=%async_computation | async-start | bytes 16777216 | tf_op jit(solution)/shard_map/all_to_all | solution.py:86
  207.0 7.8 %copy-start.4 = (s32[4]{0:T(128)S(1)}, s32[4]{0:T(128)}, u32[]{:S(2)}) copy-start(s32[4]{0:T(128)} %param.6) | copy-start | bytes 52
  207.0 50.5 %collective-permute-start = (f32[4,64,128]{2,1,0:T(8,128)S(1)}, f32[4,64,128]{2,1,0:T(8,128)S(1)}, u32[]{:S(2)}, u32[]{:S(2)}) collective-permute-start(f32[4,64,128]{2,1,0:T(8,128)S(1)} %slice.25), channel_id=1, source_target_pairs={{2,0},{4,2},{6,4},{8,6},{10,8},{12,10},{14,12},{3,1},{5,3},{7,5},{... | collective-permute-start | bytes 393224 | tf_op jit(solution)/shard_map/ppermute | solution.py:15
  212.6 2.0 copy-start.1
  402.8 7.4 %collective-permute-start.1 = (bf16[32,2048]{1,0:T(8,128)(2,1)S(1)}, bf16[32,2048]{1,0:T(8,128)(2,1)S(1)}, u32[]{:S(2)}, u32[]{:S(2)}) collective-permute-start(bf16[32,2048]{1,0:T(8,128)(2,1)S(1)} %fusion.85), channel_id=1, source_target_pairs={{0,4},{2,6},{4,8},{6,10},{8,12},{10,14},{12,0},{14,2},{1,5},{3,7},... | collective-permute-start | bytes 393224 | tf_op jit(solution)/shard_map/ppermute | solution.py:21
  422.5 8.9 %collective-permute-start.2 = (bf16[32,2048]{1,0:T(8,128)(2,1)S(1)}, bf16[32,2048]{1,0:T(8,128)(2,1)S(1)}, u32[]{:S(2)}, u32[]{:S(2)}) collective-permute-start(bf16[32,2048]{1,0:T(8,128)(2,1)S(1)} %fusion.91), channel_id=1, source_target_pairs={{0,4},{2,6},{4,8},{6,10},{8,12},{10,14},{12,0},{14,2},{1,5},{3,7},... | collective-permute-start | bytes 393224 | tf_op jit(solution)/shard_map/ppermute | solution.py:21
  443.7 7.4 %collective-permute-start.3 = (bf16[32,2048]{1,0:T(8,128)(2,1)S(1)}, bf16[32,2048]{1,0:T(8,128)(2,1)S(1)}, u32[]{:S(2)}, u32[]{:S(2)}) collective-permute-start(bf16[32,2048]{1,0:T(8,128)(2,1)S(1)} %fusion.90), channel_id=1, source_target_pairs={{0,4},{2,6},{4,8},{6,10},{8,12},{10,14},{12,0},{14,2},{1,5},{3,7},... | collective-permute-start | bytes 393224 | tf_op jit(solution)/shard_map/ppermute | solution.py:21
  463.3 7.6 %collective-permute-start.4 = (bf16[32,2048]{1,0:T(8,128)(2,1)S(1)}, bf16[32,2048]{1,0:T(8,128)(2,1)S(1)}, u32[]{:S(2)}, u32[]{:S(2)}) collective-permute-start(bf16[32,2048]{1,0:T(8,128)(2,1)S(1)} %fusion.89), channel_id=1, source_target_pairs={{0,4},{2,6},{4,8},{6,10},{8,12},{10,14},{12,0},{14,2},{1,5},{3,7},... | collective-permute-start | bytes 393224 | tf_op jit(solution)/shard_map/ppermute | solution.py:21
  483.2 7.4 %collective-permute-start.5 = (bf16[32,2048]{1,0:T(8,128)(2,1)S(1)}, bf16[32,2048]{1,0:T(8,128)(2,1)S(1)}, u32[]{:S(2)}, u32[]{:S(2)}) collective-permute-start(bf16[32,2048]{1,0:T(8,128)(2,1)S(1)} %fusion.88), channel_id=1, source_target_pairs={{0,4},{2,6},{4,8},{6,10},{8,12},{10,14},{12,0},{14,2},{1,5},{3,7},... | collective-permute-start | bytes 393224 | tf_op jit(solution)/shard_map/ppermute | solution.py:21
  502.9 7.4 %collective-permute-start.6 = (bf16[32,2048]{1,0:T(8,128)(2,1)S(1)}, bf16[32,2048]{1,0:T(8,128)(2,1)S(1)}, u32[]{:S(2)}, u32[]{:S(2)}) collective-permute-start(bf16[32,2048]{1,0:T(8,128)(2,1)S(1)} %fusion.87), channel_id=1, source_target_pairs={{0,4},{2,6},{4,8},{6,10},{8,12},{10,14},{12,0},{14,2},{1,5},{3,7},... | collective-permute-start | bytes 393224 | tf_op jit(solution)/shard_map/ppermute | solution.py:21
  522.6 7.4 %collective-permute-start.7 = (bf16[32,2048]{1,0:T(8,128)(2,1)S(1)}, bf16[32,2048]{1,0:T(8,128)(2,1)S(1)}, u32[]{:S(2)}, u32[]{:S(2)}) collective-permute-start(bf16[32,2048]{1,0:T(8,128)(2,1)S(1)} %fusion.86), channel_id=1, source_target_pairs={{0,4},{2,6},{4,8},{6,10},{8,12},{10,14},{12,0},{14,2},{1,5},{3,7},... | collective-permute-start | bytes 393224 | tf_op jit(solution)/shard_map/ppermute | solution.py:21
  530.0 6.8 %collective-permute-start.8 = (bf16[32,2048]{1,0:T(8,128)(2,1)S(1)}, bf16[32,2048]{1,0:T(8,128)(2,1)S(1)}, u32[]{:S(2)}, u32[]{:S(2)}) collective-permute-start(bf16[32,2048]{1,0:T(8,128)(2,1)S(1)} %collective-permute-done.7), channel_id=1, source_target_pairs={{0,4},{2,6},{4,8},{6,10},{8,12},{10,14},{12,0},{14,2},{1,5},{3,7},... | collective-permute-start | bytes 393224 | tf_op jit(solution)/shard_map/ppermute | solution.py:21
